TPU v7x, 32 devices: a whole 2x2x4 slice. The times are simulated.
32 devices in a mesh: node: 8 (over z, x), local: 4 (over y, core).
Axes of the slice: x: 2, y: 2, z: 4, core: 2. Of those that a mesh axis runs over, the one named last changes fastest.
Arguments:
- tokens: bfloat16 [4096, 2048], P(('node', 'local')), may hold values from -6 to 6
- expert_ids: int32 [4096, 6], P(('node', 'local')), may hold values from 0 to 15, all different within a row; in each aligned block of 128 rows (0 to 127, 128 to 255, ...) at most 82 rows name the same one
- gate_codes: int32 [4096, 6], P(('node', 'local')), may hold values from 1 to 1023
- gate_halves: bfloat16 [32, 2048, 704], P(('node', 'local')), may hold values from -0.125 to 0.125
- up_halves: bfloat16 [32, 2048, 704], P(('node', 'local')), may hold values from -0.125 to 0.125
- down_halves: bfloat16 [32, 1408, 1024], P(('node', 'local')), may hold values from -0.15625 to 0.15625
- shared_gate: bfloat16 [2048, 2816], P(None, 'local'), may hold values from -0.125 to 0.125
- shared_up: bfloat16 [2048, 2816], P(None, 'local'), may hold values from -0.125 to 0.125
- shared_down: bfloat16 [2816, 2048], P('local'), may hold values from -0.109375 to 0.109375
Outputs:
- mixed: bfloat16 [4096, 2048], P(('node', 'local'))
Inputs may be any that keep to these rules, and one draw needn't show every extreme that they name: `expert_ids`: the experts of one token differ. Among the rows of one device, no expert is named more than 82 times, a bound that some block reaches; every expert is named somewhere.
All inputs are finite; a program needn't handle non-finite values.
Results may differ from a plain program's by a relative error of at most 0.01.
Values may be sent and summed in bfloat16 or wider, within the bound.
A program may use at most 128 MiB of HBM per device.

v0:
```python
import jax
import jax.numpy as jnp
from jax import lax
from jax.sharding import PartitionSpec as P


def from_partner(block, axis, distance):
    count = lax.axis_size(axis)
    route = []
    for low in range(count):
        high = low | 1 << distance
        if high != low and high < count:
            route += [(low, high), (high, low)]
    return lax.ppermute(block, axis, route)


def dispatch(send_block):
    return lax.all_to_all(send_block, ("node", "local"), split_axis=0, concat_axis=0, tiled=True)


def combine(send_block):
    return lax.all_to_all(send_block, ("node", "local"), split_axis=0, concat_axis=0, tiled=True)


def half_hidden(received, gate_half, up_half, dtype):
    expert_rows = received.reshape(-1, received.shape[-1])
    gate_out = jnp.dot(expert_rows, gate_half, preferred_element_type=jnp.float32)
    up_out = jnp.dot(expert_rows, up_half, preferred_element_type=jnp.float32)
    return (jax.nn.silu(gate_out) * up_out).astype(dtype)


def side_by_side(own_part, other_part, parity, axis):
    lower = jnp.where(parity == 0, own_part, other_part)
    upper = jnp.where(parity == 0, other_part, own_part)
    return jnp.concatenate([lower, upper], axis=axis)


def local(
    tokens,
    expert_ids,
    gate_codes,
    gate_halves,
    up_halves,
    down_halves,
    shared_gate,
    shared_up,
    shared_down,
):
    tok_rows, features = tokens.shape
    fanout = expert_ids.shape[1]
    devices = lax.axis_size("node") * lax.axis_size("local")
    experts = devices // 2
    capacity = 2 * (5 * tok_rows * fanout // (6 * experts) + 1)
    parity = lax.axis_index("local") % 2
    flat_ids = expert_ids.reshape(-1)
    onehot = (flat_ids[:, None] == jnp.arange(experts, dtype=jnp.int32)[None, :]).astype(jnp.int32)
    slot_index = jnp.sum((jnp.cumsum(onehot, axis=0) - 1) * onehot, axis=1)
    dest_row = flat_ids * capacity + slot_index
    owner_row = jnp.arange(tok_rows * fanout, dtype=jnp.int32) // fanout
    buffer = (
        jnp.zeros((experts * capacity, features), tokens.dtype).at[dest_row].set(tokens[owner_row])
    )
    codes = gate_codes.astype(jnp.float32)
    weights = (codes / jnp.sum(codes, axis=1, keepdims=True)).reshape(-1)
    send_block = jnp.broadcast_to(
        buffer.reshape(experts, 1, capacity, features), (experts, 2, capacity, features)
    ).reshape(devices, capacity, features)
    received = dispatch(send_block)
    hidden_own = half_hidden(received, gate_halves[0], up_halves[0], tokens.dtype)
    hidden_other = from_partner(hidden_own, "local", 0)
    hidden = side_by_side(hidden_own, hidden_other, parity, 1)
    result = jnp.dot(hidden, down_halves[0], preferred_element_type=jnp.float32).astype(
        tokens.dtype
    )
    returned = combine(result.reshape(devices, capacity, features // 2))
    outputs = (
        returned.reshape(experts, 2, capacity, features // 2)
        .transpose(0, 2, 1, 3)
        .reshape(experts * capacity, features)
    )
    picked = outputs[dest_row].astype(jnp.float32) * weights[:, None]
    routed = jnp.sum(picked.reshape(tok_rows, fanout, features), axis=1)
    block_rows = lax.all_gather(tokens, "local", axis=0, tiled=True)
    gate_part = jnp.dot(block_rows, shared_gate, preferred_element_type=jnp.float32)
    up_part = jnp.dot(block_rows, shared_up, preferred_element_type=jnp.float32)
    shared_hidden = (jax.nn.silu(gate_part) * up_part).astype(tokens.dtype)
    block_rows = shared_hidden
    shared_out = lax.psum_scatter(
        jnp.dot(block_rows, shared_down, preferred_element_type=jnp.float32).astype(jnp.bfloat16),
        "local",
        scatter_dimension=0,
        tiled=True,
    ).astype(jnp.float32)
    return (routed + shared_out).astype(tokens.dtype)


def solution(mesh):
    in_specs = (
        P(("node", "local"), None),
        P(("node", "local"), None),
        P(("node", "local"), None),
        P(("node", "local"), None, None),
        P(("node", "local"), None, None),
        P(("node", "local"), None, None),
        P(None, "local"),
        P(None, "local"),
        P("local", None),
    )
    out_specs = P(("node", "local"), None)
    return jax.shard_map(local, mesh=mesh, in_specs=in_specs, out_specs=out_specs, check_vma=False)
```

profile of v0, /device:TPU:0, one launch (start us, length us, event | category | flops | bytes accessed | tf_op | source)
XLA Modules:
  0.0 567.3 jit_solution(16868494774283275314)
XLA Ops:
  6.5 0.8 broadcast_multiply_fusion
  7.4 0.8 copy.13
  8.2 0.1 eq.32
  8.3 0.1 eq.36
  8.6 0.1 mul.44
  8.8 1.7 reduce-window.6
  10.5 0.3 slice_reduce_fusion
  10.9 32.0 %scatter_custom_fusion = bf16[1312,2048]{1,0:T(8,128)(2,1)} fusion(s32[768]{0:T(1024)S(1)} %fusion.18, bf16[128,2048]{1,0:T(8,128)(2,1)} %param.9, s32[1024]{0:T(1024)S(1)} %pad_clamp_fusion.1, bf16[]{:T(256)} %constant.41.clone.1), kind=kCustom, calls=%fused_computation.12 | custom fusion | bytes 5374464 | tf_op jit(solution)/shard_map/scatter | solution.py:61
  42.9 6.0 %broadcast_in_dim.7 = bf16[16,82,2048]{2,1,0:T(8,128)(2,1)} reshape(bf16[1312,2048]{1,0:T(8,128)(2,1)} %scatter_custom_fusion) | data formatting | bytes 10747904 | tf_op jit(solution)/shard_map/broadcast_in_dim | solution.py:65
  48.9 5.0 broadcast_in_dim.8
  53.9 258.2 %all_to_all.10 = bf16[32,82,2048]{2,1,0:T(8,128)(2,1)} all-to-all(bf16[32,82,2048]{2,1,0:T(8,128)(2,1)S(1)} %bitcast.39), channel_id=1, replica_groups=mesh['node'=8,'local'=4] {'node','local'}, dimensions={0} | all-to-all | bytes 21495808 | tf_op jit(solution)/shard_map/all_to_all | solution.py:18
  312.1 11.4 %reshape.121 = bf16[2624,2048]{1,0:T(8,128)(2,1)} reshape(bf16[32,82,2048]{2,1,0:T(8,128)(2,1)} %all_to_all.10) | data formatting | bytes 21495808 | tf_op jit(solution)/shard_map/reshape | solution.py:26
  323.5 15.2 %fusion.11 = f32[2624,704]{0,1:T(8,128)} fusion(bf16[2624,2048]{1,0:T(8,128)(2,1)} %reshape.121, bf16[1,2048,704]{1,2,0:T(8,128)(2,1)} %param.12), kind=kOutput, calls=%fused_computation.17 | convolution fusion | flops 7566524416 | bytes 21020672 | tf_op jit(solution)/shard_map/dot_general | solution.py:27
  338.8 17.9 %multiply_convert_fusion = bf16[2624,704]{0,1:T(8,128)(2,1)} fusion(f32[2624,704]{0,1:T(8,128)} %fusion.11, bf16[2624,2048]{1,0:T(8,128)(2,1)S(1)} %copy-done.2, bf16[1,2048,704]{1,2,0:T(8,128)(2,1)S(1)} %copy-done.4), kind=kOutput, calls=%fused_computation.8 | convolution fusion | flops 7577608192 | bytes 24715264 | tf_op jit(solution)/shard_map/dot_general | solution.py:28
  356.7 6.9 %collective-permute-done = bf16[2624,704]{0,1:T(8,128)(2,1)} collective-permute-done((bf16[2624,704]{0,1:T(8,128)(2,1)}, bf16[2624,704]{0,1:T(8,128)(2,1)}, u32[]{:S(2)}, u32[]{:S(2)}) %collective-permute-start) | collective-permute-done | bytes 3694624 | tf_op jit(solution)/shard_map/ppermute | solution.py:14
  363.6 3.6 broadcast_select_fusion.1
  367.2 10.8 %fusion.4 = bf16[2624,1024]{1,0:T(8,128)(2,1)} fusion(bf16[2624,704]{0,1:T(8,128)(2,1)S(1)} %get-tuple-element.6, bf16[2624,704]{0,1:T(8,128)(2,1)S(1)} %get-tuple-element.5, bf16[1,1408,1024]{2,1,0:T(8,128)(2,1)S(1)} %copy-done), kind=kOutput, calls=%fused_computation.9 | convolution fusion | flops 7583989760 | bytes 15646720 | tf_op jit(solution)/shard_map/dot_general | solution.py:72
  378.0 7.8 %reshape.122 = bf16[32,82,1024]{2,1,0:T(8,128)(2,1)} reshape(bf16[2624,1024]{1,0:T(8,128)(2,1)} %fusion.4) | data formatting | bytes 10747904 | tf_op jit(solution)/shard_map/reshape | solution.py:75
  385.7 4.0 all-to-all-start.1
  389.8 0.7 all-gather.2.cloned.1.call-update
  390.5 10.3 %reduce-scatter.2.cloned.1.call-start = ((), (), s32[]{:S(2)}) async-start(), calls=%async_computation.4 | async-start | bytes 2621440 | tf_op jit(solution)/shard_map/reduce_scatter | solution.py:88
  400.8 44.5 %all-gather.2.cloned.1.call-done = bf16[512,2048]{1,0:T(8,128)(2,1)} async-done(((bf16[128,2048]{1,0:T(8,128)(2,1)}), bf16[512,2048]{1,0:T(8,128)(2,1)}) %all-gather.2.cloned.1.call-update) | async-done | bytes 2097168 | tf_op jit(solution)/shard_map/all_gather | solution.py:83
  445.3 4.4 fusion.22
  449.6 8.6 %convolution_convert_fusion = bf16[512,2048]{1,0:T(8,128)(2,1)} fusion(bf16[704,2048]{1,0:T(8,128)(2,1)} %param.17, bf16[512,2048]{1,0:T(8,128)(2,1)} %all-gather.2.cloned.1.call-done, bf16[2048,704]{0,1:T(8,128)(2,1)} %param.16, f32[512,704]{0,1:T(8,128)} %fusion.22), kind=kOutput, calls=%fused_computation.14 | convolution fusion | flops 2956001280 | bytes 11403264 | tf_op jit(solution)/shard_map/dot_general | solution.py:89
  458.3 0.1 copy.17
  458.4 60.1 %all-to-all-done.1 = bf16[32,82,1024]{2,1,0:T(8,128)(2,1)} async-done(((bf16[32,82,1024]{2,1,0:T(8,128)(2,1)}), bf16[32,82,1024]{2,1,0:T(8,128)(2,1)}, u32[]{:S(2)}, u32[]{:S(2)}) %all-to-all-start.1) | async-done | bytes 5373984 | tf_op jit(solution)/shard_map/all_to_all | solution.py:22
  518.5 10.3 %copy.16 = bf16[16,2,82,1024]{3,1,2,0:T(2,128)(2,1)S(1)} copy(bf16[16,2,82,1024]{3,2,1,0:T(8,128)(2,1)} %bitcast.5) | data formatting | bytes 10747904 | tf_op jit(solution)/shard_map/reshape | solution.py:77
  528.9 4.6 copy.19
  533.4 10.3 %gather_fusion = bf16[768,2048]{1,0:T(8,128)(2,1)} fusion(bf16[1312,2048]{1,0:T(8,128)(2,1)} %bitcast.38, s32[1024]{0:T(1024)S(1)} %pad_clamp_fusion), kind=kCustom, calls=%fused_computation.1 | custom fusion | bytes 6294528 | tf_op jit(solution)/shard_map/gather | solution.py:81
  543.7 6.7 %reshape.125 = f32[128,6,2048]{2,1,0:T(8,128)} reshape(bf16[768,2048]{1,0:T(8,128)(2,1)} %gather_fusion) | data formatting | bytes 9437184 | tf_op jit(solution)/shard_map/convert_element_type | solution.py:81
  550.4 7.6 %multiply_reduce_fusion = f32[128,2048]{1,0:T(8,128)} fusion(f32[128,6,2048]{2,1,0:T(8,128)} %reshape.125, f32[128,6]{1,0:T(8,128)S(1)} %copy.17), kind=kLoop, calls=%fused_computation.3 | loop fusion | flops 2883584 | bytes 7343104 | tf_op jit(solution)/shard_map/reduce_sum | solution.py:82
  558.0 2.3 add_convert_fusion
  (26 shorter events, 0.4 us)
Async XLA Ops:
  6.5 360.6 %copy-start = (bf16[1,1408,1024]{2,1,0:T(8,128)(2,1)S(1)}, bf16[1,1408,1024]{2,1,0:T(8,128)(2,1)}, u32[]{:S(2)}) copy-start(bf16[1,1408,1024]{2,1,0:T(8,128)(2,1)} %param.14) | copy-start | bytes 8650756
  323.5 15.2 %copy-start.2 = (bf16[2624,2048]{1,0:T(8,128)(2,1)S(1)}, bf16[2624,2048]{1,0:T(8,128)(2,1)}, u32[]{:S(2)}) copy-start(bf16[2624,2048]{1,0:T(8,128)(2,1)} %reshape.121) | copy-start | bytes 32243716
  323.5 15.2 %copy-start.4 = (bf16[1,2048,704]{1,2,0:T(8,128)(2,1)S(1)}, bf16[1,2048,704]{1,2,0:T(8,128)(2,1)}, u32[]{:S(2)}) copy-start(bf16[1,2048,704]{1,2,0:T(8,128)(2,1)} %param.13) | copy-start | bytes 8650756
  356.7 6.9 %collective-permute-start = (bf16[2624,704]{0,1:T(8,128)(2,1)}, bf16[2624,704]{0,1:T(8,128)(2,1)}, u32[]{:S(2)}, u32[]{:S(2)}) collective-permute-start(bf16[2624,704]{0,1:T(8,128)(2,1)} %multiply_convert_fusion), channel_id=1, source_target_pairs={{0,1},{1,0},{2,3},{3,2},{4,5},{5,4},{6,7},{7,6},{8,9},{9,8},{10,11... | collective-permute-start | bytes 11083784 | tf_op jit(solution)/shard_map/ppermute | solution.py:14
  385.7 59.5 %copy-start.5 = (bf16[2048,704]{0,1:T(8,128)(2,1)S(1)}, bf16[2048,704]{0,1:T(8,128)(2,1)}, u32[]{:S(2)}) copy-start(bf16[2048,704]{0,1:T(8,128)(2,1)} %param.15) | copy-start | bytes 8650756
  385.7 132.8 %all-to-all-start.1 = ((bf16[32,82,1024]{2,1,0:T(8,128)(2,1)}), bf16[32,82,1024]{2,1,0:T(8,128)(2,1)}, u32[]{:S(2)}, u32[]{:S(2)}) async-start(bf16[32,82,1024]{2,1,0:T(8,128)(2,1)} %reshape.122), calls=%async_computation.1 | async-start | bytes 11534336 | tf_op jit(solution)/shard_map/all_to_all | solution.py:22
  389.8 55.5 %all-gather.2.cloned.1.call-start = ((), (), s32[]{:S(2)}) async-start(), calls=%async_computation.3 | async-start | bytes 2621440 | tf_op jit(solution)/shard_map/all_gather | solution.py:83
  390.5 167.5 %reduce-scatter.2.cloned.1.call-start = ((), (), s32[]{:S(2)}) async-start(), calls=%async_computation.4 | async-start | bytes 2621440 | tf_op jit(solution)/shard_map/reduce_scatter | solution.py:88
  449.6 8.6 %copy-start.3 = (s32[128,6]{0,1:T(8,128)S(1)}, s32[128,6]{0,1:T(8,128)}, u32[]{:S(2)}) copy-start(s32[128,6]{0,1:T(8,128)} %param.11) | copy-start | bytes 9220
  543.7 16.6 %copy-start.1 = (bf16[1,1408,1024]{2,1,0:T(8,128)(2,1)S(1)}, bf16[1,1408,1024]{2,1,0:T(8,128)(2,1)}, u32[]{:S(2)}) copy-start(bf16[1,1408,1024]{2,1,0:T(8,128)(2,1)} %param.14) | copy-start | bytes 8650756
Sparse Core Ops, SparseCore 0:
  392.2 53.0 all-gather.1
  458.4 45.7 reduce-scatter.1
where the time goes:
time: 577 us; the launch traced here: 567 us
  blocking collectives  258 us (45%)
  waiting for transfers between devices  112 us (19%)
  local copies, waits for them, and re-layouts  95.8 us (17%)
  matrix products  56.9 us (10%)
  other arithmetic  16.2 us (3%)
  starting transfers between devices  14.3 us (2%)
  between operations  13.7 us (2%)
    all_to_all x1, blocking collectives, dispatch(): lax.all_to_all(send_block, ('node', 'local'), split_axis=0, concat_axis=0...  258 us
    all_to_all x1, waiting for transfers between devices, combine(): lax.all_to_all(send_block, ('node', 'local'), split_axis=0, concat_axis=0...  60.1 us
    all_gather x1, waiting for transfers between devices, local(): block_rows = lax.all_gather(tokens, 'local', axis=0, tiled=True)  44.5 us
    scatter x1, local copies, waits for them, and re-layouts, local(): jnp.zeros((experts * capacity, features), tokens.dtype).at[dest_row]  32 us
    dot_general x1, matrix products, half_hidden(): up_out = jnp.dot(expert_rows, up_half, preferred_element_type=jnp.float32)  17.9 us
    dot_general x1, matrix products, half_hidden(): jnp.dot(expert_rows, gate_half, preferred_element_type=jnp.float32)  15.2 us
  transfers between devices with their start and end apart: 4, of which 3 were waited for; matrix products, arithmetic and copies ran while one was open for 9% of the time, Pallas kernels for 0%

commit v1 on v0

--- a/solution.py
+++ b/solution.py
@@ -93,18 +93,111 @@
     ).astype(jnp.float32)
     return (routed + shared_out).astype(tokens.dtype)
 
+def swap_cores(block):
+    return lax.ppermute(block, "core", [(0, 1), (1, 0)])
+
+
+def both_halves(block, core):
+    other = swap_cores(block)
+    return jnp.where(core == 0, block, other), jnp.where(core == 0, other, block)
+
+
+def dense(
+    tokens,
+    expert_ids,
+    gate_codes,
+    gate_halves,
+    up_halves,
+    down_halves,
+    shared_gate,
+    shared_up,
+    shared_down,
+):
+    rows, features = tokens.shape
+    planes = ("node", "chip")
+    chips = lax.axis_size("node") * lax.axis_size("chip")
+    group_chips = lax.axis_size("chip")
+    core = lax.axis_index("core")
+    chip = lax.axis_index("chip")
+    node = lax.axis_index("node")
+    expert = node * group_chips + chip
+
+    codes = gate_codes.astype(jnp.float32)
+    weights = codes / jnp.sum(codes, axis=1, keepdims=True)
+    onehot = expert_ids[:, :, None] == jnp.arange(chips, dtype=jnp.int32)[None, None, :]
+    table = jnp.sum(jnp.where(onehot, weights[:, :, None], 0.0), axis=1)
+
+    plane_rows = lax.all_gather(tokens, planes, axis=0, tiled=True)
+    share = lax.all_to_all(table.T.reshape(chips, 1, rows), planes, split_axis=0, concat_axis=0, tiled=True)
+    scale = share.reshape(-1, 1)
+
+    gate = both_halves(gate_halves[0], core)
+    up = both_halves(up_halves[0], core)
+    down = both_halves(down_halves[0], core)
+
+    group = lax.all_gather(lax.all_gather(tokens, "chip", axis=0, tiled=True), "core", axis=0, tiled=True)
+    shared_hidden = (
+        jax.nn.silu(jnp.dot(group, shared_gate, preferred_element_type=jnp.float32))
+        * jnp.dot(group, shared_up, preferred_element_type=jnp.float32)
+    ).astype(tokens.dtype)
+    shared_rows = jnp.dot(shared_hidden, shared_down, preferred_element_type=jnp.float32)
+    shared_rows = shared_rows.astype(tokens.dtype).reshape(2, group_chips * rows, features)
+    mine = jnp.where(core == 0, shared_rows[0], shared_rows[1])
+    theirs = jnp.where(core == 0, shared_rows[1], shared_rows[0])
+    shared_part = mine.astype(jnp.float32) + swap_cores(theirs).astype(jnp.float32)
+
+    hidden = jnp.concatenate(
+        [
+            (
+                jax.nn.silu(jnp.dot(plane_rows, gate[h], preferred_element_type=jnp.float32))
+                * jnp.dot(plane_rows, up[h], preferred_element_type=jnp.float32)
+            ).astype(tokens.dtype)
+            for h in (0, 1)
+        ],
+        axis=1,
+    )
+    out = jnp.concatenate(
+        [
+            (jnp.dot(hidden, down[h], preferred_element_type=jnp.float32) * scale).astype(tokens.dtype)
+            for h in (0, 1)
+        ],
+        axis=1,
+    )
+    first = node * group_chips * rows
+    block = lax.dynamic_slice(out, (first, 0), (group_chips * rows, features))
+    block = (block.astype(jnp.float32) + shared_part).astype(tokens.dtype)
+    out = lax.dynamic_update_slice(out, block, (first, 0))
+    return lax.psum_scatter(out, planes, scatter_dimension=0, tiled=True)
+
+
+def program(mesh, row, pieces, body):
+    in_specs = (
+        P(row, None),
+        P(row, None),
+        P(row, None),
+        P(row, None, None),
+        P(row, None, None),
+        P(row, None, None),
+        P(None, pieces),
+        P(None, pieces),
+        P(pieces, None),
+    )
+    return jax.shard_map(
+        body, mesh=mesh, in_specs=in_specs, out_specs=P(row, None), check_vma=False
+    )
+
 
 def solution(mesh):
-    in_specs = (
-        P(("node", "local"), None),
-        P(("node", "local"), None),
-        P(("node", "local"), None),
-        P(("node", "local"), None, None),
-        P(("node", "local"), None, None),
-        P(("node", "local"), None, None),
-        P(None, "local"),
-        P(None, "local"),
-        P("local", None),
-    )
-    out_specs = P(("node", "local"), None)
-    return jax.shard_map(local, mesh=mesh, in_specs=in_specs, out_specs=out_specs, check_vma=False)
+    experts = mesh.devices.size // 2
+    fine = jax.sharding.Mesh(
+        mesh.devices.reshape(mesh.devices.shape[0], -1, 2), ("node", "chip", "core")
+    )
+
+    def run(tokens, expert_ids, *others):
+        if experts <= 4 * expert_ids.shape[1]:
+            whole = program(fine, ("node", "chip", "core"), ("chip", "core"), dense)
+        else:
+            whole = program(mesh, ("node", "local"), "local", local)
+        return whole(tokens, expert_ids, *others)
+
+    return run

time: 577 us -> 434 us (0.75); the launches traced: 567 us -> 434 us
  blocking collectives: 258 us -> 0 us
  waiting for transfers between devices: 112 us -> 310 us
  local copies, waits for them, and re-layouts: 95.8 us -> 12.3 us
  matrix products: 56.9 us -> 74.9 us
  starting transfers between devices: 14.3 us -> 6.59 us
    all_to_all x1 -> x0, blocking collectives: 258 us -> none  [dispatch(): lax.all_to_all(send_block, ('node', 'local'), split_axis=0, concat_axis=0...]
    reduce_scatter x1, waiting for transfers between devices: 0.01 us -> 177 us  [dense(): return lax.psum_scatter(out, planes, scatter_dimension=0, tiled=True)]
    all_gather x1 -> x3, waiting for transfers between devices: 44.5 us -> 131 us  [the longest x1 99.6 us: dense(): plane_rows = lax.all_gather(tokens, planes, axis=0, tiled=True)]
    all_to_all x1, waiting for transfers between devices: 60.1 us -> 0.01 us  [dense(): lax.all_to_all(table.T.reshape(chips, 1, rows), planes, split_axis=0, con...]
    scatter x1 -> x0, local copies, waits for them, and re-layouts: 32 us -> none  [local(): jnp.zeros((experts * capacity, features), tokens.dtype).at[dest_row]]
    reshape x3 -> x0, local copies, waits for them, and re-layouts: 29.5 us -> none  [the longest x1 11.4 us: half_hidden(): expert_rows = received.reshape(-1, received.shape[-1])]
    dot_general x5 -> x8, matrix products: 56.9 us -> 74.9 us  [the longest x2 21.7 us: dense(): jnp.dot(hidden, down[h], preferred_element_type=jnp.float32) * scale]
    broadcast_in_dim x2 -> x0, local copies, waits for them, and re-layouts: 11 us -> none  [local(): jnp.broadcast_to(buffer.reshape(experts, 1, capacity, features), (experts...]
  transfers between devices with their start and end apart: 4 -> 9, of which waited for: 3 -> 4; matrix products, arithmetic and copies ran while one was open for 9% -> 20% of each run, Pallas kernels for 0% -> 0%
where the time goes in v1:
time: 434 us
  waiting for transfers between devices  310 us (71%)
  matrix products  74.9 us (17%)
  other arithmetic  17.1 us (4%)
  between operations  13.2 us (3%)
  local copies, waits for them, and re-layouts  12.3 us (3%)
  starting transfers between devices  6.59 us (2%)
    reduce_scatter x1, waiting for transfers between devices, dense(): return lax.psum_scatter(out, planes, scatter_dimension=0, tiled=True)  177 us
    all_gather x1, waiting for transfers between devices, dense(): plane_rows = lax.all_gather(tokens, planes, axis=0, tiled=True)  99.6 us
    all_gather x1, waiting for transfers between devices, dense(): lax.all_gather(tokens, 'chip', axis=0, tiled=True)  25.6 us
    dot_general x2, matrix products, dense(): jnp.dot(hidden, down[h], preferred_element_type=jnp.float32) * scale  21.7 us
    dot_general x2, matrix products, dense(): jnp.dot(plane_rows, up[h], preferred_element_type=jnp.float32)  20.7 us
    dot_general x2, matrix products, dense(): jnp.dot(plane_rows, gate[h], preferred_element_type=jnp.float32)  19.5 us
    unnamed x19, local copies, waits for them, and re-layouts  12.3 us
  transfers between devices with their start and end apart: 9, of which 4 were waited for; matrix products, arithmetic and copies ran while one was open for 20% of the time, Pallas kernels for 0%

profile of v1, /device:TPU:0, one launch (start us, length us, event | category | flops | bytes accessed | tf_op | source)
XLA Modules:
  0.0 433.9 jit_solution(12615217622593558698)
XLA Ops:
  6.5 0.7 all-gather.6.cloned.1.call-update
  7.3 0.0 all-gather.8.cloned.1.call-start
  7.3 25.6 %all-gather.6.cloned.1.call-done = bf16[256,2048]{1,0:T(8,128)(2,1)} async-done(((bf16[128,2048]{1,0:T(8,128)(2,1)}), bf16[256,2048]{1,0:T(8,128)(2,1)}) %all-gather.6.cloned.1.call-update) | async-done | bytes 1048592 | tf_op jit(solution)/shard_map/all_gather | solution.py:138
  32.9 0.0 all-gather.8.cloned.1.call-update
  33.0 0.0 all-gather.4.cloned.1.call-start
  33.0 0.7 all-gather.4.cloned.1.call-update
  33.7 0.1 collective-permute-start
  33.8 0.5 collective-permute-start.1
  34.3 0.1 collective-permute-start.2
  34.4 0.7 convert_reduce_fusion
  35.1 0.7 convert_divide_fusion
  35.8 1.3 select_reduce_fusion
  37.1 5.6 %all-to-all-start = ((f32[16,1,128]{2,1,0:T(1,128)}), f32[16,1,128]{2,1,0:T(1,128)S(1)}, u32[]{:S(2)}, u32[]{:S(2)}) async-start(f32[16,1,128]{2,1,0:T(1,128)} %bitcast.9), calls=%async_computation | async-start | bytes 16384 | tf_op jit(solution)/shard_map/all_to_all | solution.py:131
  42.7 0.0 reduce-scatter.4.cloned.1.call-start
  42.7 6.2 %all-gather.8.cloned.1.call-done = bf16[512,2048]{1,0:T(8,128)(2,1)} async-done(((bf16[256,2048]{1,0:T(8,128)(2,1)}), bf16[512,2048]{1,0:T(8,128)(2,1)}) %all-gather.8.cloned.1.call-update) | async-done | bytes 2097168 | tf_op jit(solution)/shard_map/all_gather | solution.py:138
  49.0 5.3 %fusion.34 = f32[512,704]{0,1:T(8,128)} fusion(bf16[512,2048]{1,0:T(8,128)(2,1)} %all-gather.8.cloned.1.call-done, bf16[2048,704]{0,1:T(8,128)(2,1)} %param.15), kind=kOutput, calls=%fused_computation.54 | convolution fusion | flops 1476395008 | bytes 6422528 | tf_op jit(solution)/shard_map/dot_general | solution.py:140
  54.2 7.7 %convolution_convert_fusion = bf16[512,2048]{0,1:T(8,128)(2,1)} fusion(bf16[704,2048]{1,0:T(8,128)(2,1)S(1)} %copy-done, bf16[512,2048]{1,0:T(8,128)(2,1)} %all-gather.8.cloned.1.call-done, bf16[2048,704]{0,1:T(8,128)(2,1)} %param.16, f32[512,704]{0,1:T(8,128)} %fusion.34), kind=kOutput, calls=%fused_computation.20 | convolution fusion | flops 2956001280 | bytes 11403264 | tf_op jit(solution)/shard_map/dot_general | solution.py:143
  61.9 2.8 broadcast_select_fusion
  64.7 0.2 collective-permute-start.3
  64.9 99.6 %all-gather.4.cloned.1.call-done = bf16[2048,2048]{1,0:T(8,128)(2,1)} async-done(((bf16[128,2048]{1,0:T(8,128)(2,1)}), bf16[2048,2048]{1,0:T(8,128)(2,1)}) %all-gather.4.cloned.1.call-update) | async-done | bytes 8388624 | tf_op jit(solution)/shard_map/all_gather | solution.py:130
  164.5 11.5 %fusion.11 = f32[704,2048]{1,0:T(8,128)} fusion(bf16[2048,2048]{1,0:T(8,128)(2,1)} %all-gather.4.cloned.1.call-done, bf16[2048,704]{0,1:T(8,128)(2,1)} %collective-permute-done, pred[]{:T(512)S(6)} %eq.8, bf16[1,2048,704]{1,2,0:T(8,128)(2,1)S(1)} %copy-done.4), kind=kOutput, calls=%fused_computation.24 | convolution fusion | flops 5907021824 | bytes 19922944 | tf_op jit(solution)/shard_map/dot_general | solution.py:152
  176.0 0.0 collective-permute-done.1
  176.0 10.7 %fusion = bf16[2048,704]{0,1:T(8,128)(2,1)} fusion(f32[704,2048]{1,0:T(8,128)} %fusion.11, bf16[2048,2048]{1,0:T(8,128)(2,1)S(1)} %copy-done.3, bf16[2048,704]{0,1:T(8,128)(2,1)} %collective-permute-done.1, pred[]{:T(512)S(6)} %eq.8, bf16[1,2048,704]{1,2,0:T(8,128)(2,1)S(1)} %copy-done.5), kind=kOutput, calls=%fused_computation.7 | convolution fusion | flops 5915672576 | bytes 22806528 | tf_op jit(solution)/shard_map/dot_general | solution.py:153
  186.8 8.0 %fusion.14 = f32[704,2048]{1,0:T(8,128)} fusion(bf16[2048,2048]{1,0:T(8,128)(2,1)S(1)} %copy-done.3, bf16[2048,704]{0,1:T(8,128)(2,1)} %collective-permute-done, pred[]{:T(512)S(6)} %eq.8, bf16[1,2048,704]{1,2,0:T(8,128)(2,1)S(1)} %copy-done.4), kind=kOutput, calls=%fused_computation.27 | convolution fusion | flops 5907021824 | bytes 19922944 | tf_op jit(solution)/shard_map/dot_general | solution.py:152
  194.8 10.0 %fusion.4 = bf16[2048,704]{0,1:T(8,128)(2,1)} fusion(f32[704,2048]{1,0:T(8,128)} %fusion.14, bf16[2048,2048]{1,0:T(8,128)(2,1)S(1)} %copy-done.3, bf16[2048,704]{0,1:T(8,128)(2,1)} %collective-permute-done.1, pred[]{:T(512)S(6)} %eq.8, bf16[1,2048,704]{1,2,0:T(8,128)(2,1)S(1)} %copy-done.5), kind=kOutput, calls=%fused_computation.14 | convolution fusion | flops 5915672576 | bytes 22806528 | tf_op jit(solution)/shard_map/dot_general | solution.py:153
  204.8 11.5 %multiply_convert_fusion.1 = bf16[2048,1024]{0,1:T(8,128)(2,1)} fusion(f32[2048]{0:T(1024)S(1)} %bitcast.77, bf16[2048,704]{0,1:T(8,128)(2,1)} %fusion, bf16[2048,704]{0,1:T(8,128)(2,1)} %fusion.4, bf16[1408,1024]{1,0:T(8,128)(2,1)} %collective-permute-done.2, pred[]{:T(512)S(6)} %eq.8, bf16[1,1408,1024]{2,1,0:T(8,128)(2,1)S(1)} %copy-done.6), kind=kOutput, calls=%fused_computation.4 | convolution fusion | flops 5922750464 | bytes 15736833 | tf_op jit(solution)/shard_map/dot_general | solution.py:161
  216.3 10.2 %multiply_convert_fusion = bf16[2048,1024]{0,1:T(8,128)(2,1)} fusion(f32[2048]{0:T(1024)S(1)} %bitcast.78, bf16[2048,704]{0,1:T(8,128)(2,1)S(1)} %copy-done.7, bf16[2048,704]{0,1:T(8,128)(2,1)S(1)} %copy-done.8, bf16[1408,1024]{1,0:T(8,128)(2,1)} %collective-permute-done.2, pred[]{:T(512)S(6)} %eq.8, bf16[1,1408,1024]{2,1,0:T(8,128)(2,1)S(1)} %copy-done.6), kind=kOutput, calls=%fused_computation.3 | convolution fusion | flops 5922750464 | bytes 15736833 | tf_op jit(solution)/shard_map/dot_general | solution.py:161
  226.5 8.5 %pad_maximum_fusion = bf16[2048,2048]{0,1:T(8,128)(2,1)} fusion(bf16[2048,1024]{0,1:T(8,128)(2,1)} %multiply_convert_fusion, bf16[2048,1024]{0,1:T(8,128)(2,1)} %multiply_convert_fusion.1), kind=kLoop, calls=%fused_computation.1 | loop fusion | flops 16777216 | bytes 16777216 | tf_op jit(solution)/shard_map/concatenate | solution.py:159
  235.1 3.0 fusion.24
  238.1 12.3 %copy.26 = bf16[2048,2048]{1,0:T(8,128)(2,1)} copy(bf16[2048,2048]{0,1:T(8,128)(2,1)} %fusion.24) | data formatting | bytes 16777216
  250.4 0.0 reduce-scatter.4.cloned.1.call-update
  250.5 176.9 %reduce-scatter.4.cloned.1.call-done = bf16[128,2048]{1,0:T(8,128)(2,1)} async-done(((bf16[2048,2048]{1,0:T(8,128)(2,1)}), bf16[128,2048]{1,0:T(8,128)(2,1)}) %reduce-scatter.4.cloned.1.call-update) | async-done | bytes 524304 | tf_op jit(solution)/shard_map/reduce_scatter | solution.py:170
  (23 shorter events, 0.0 us)
Async XLA Ops:
  6.5 47.7 %copy-start = (bf16[704,2048]{1,0:T(8,128)(2,1)S(1)}, bf16[704,2048]{1,0:T(8,128)(2,1)}, u32[]{:S(2)}) copy-start(bf16[704,2048]{1,0:T(8,128)(2,1)} %param.17) | copy-start | bytes 8650756
  6.5 26.4 %all-gather.6.cloned.1.call-start = ((), (), s32[]{:S(2)}) async-start(), calls=%async_computation.3 | async-start | bytes 1572864 | tf_op jit(solution)/shard_map/all_gather | solution.py:138
  7.3 41.7 %all-gather.8.cloned.1.call-start = ((), (), s32[]{:S(2)}) async-start(), calls=%async_computation.4 | async-start | bytes 3145728 | tf_op jit(solution)/shard_map/all_gather | solution.py:138
  33.0 131.6 %all-gather.4.cloned.1.call-start = ((), (), s32[]{:S(2)}) async-start(), calls=%async_computation.2 | async-start | bytes 8912896 | tf_op jit(solution)/shard_map/all_gather | solution.py:130
  33.7 31.2 %collective-permute-start = (bf16[2048,704]{0,1:T(8,128)(2,1)}, bf16[2048,704]{0,1:T(8,128)(2,1)}, u32[]{:S(2)}, u32[]{:S(2)}) collective-permute-start(bf16[2048,704]{0,1:T(8,128)(2,1)} %bitcast.79), channel_id=1, source_target_pairs={{0,1},{1,0},{2,3},{3,2},{4,5},{5,4},{6,7},{7,6},{8,9},{9,8},{10,11... | collective-permute-start | bytes 8650760 | tf_op jit(solution)/shard_map/ppermute | solution.py:97
  33.8 142.2 %collective-permute-start.1 = (bf16[2048,704]{0,1:T(8,128)(2,1)}, bf16[2048,704]{0,1:T(8,128)(2,1)}, u32[]{:S(2)}, u32[]{:S(2)}) collective-permute-start(bf16[2048,704]{0,1:T(8,128)(2,1)} %bitcast.80), channel_id=1, source_target_pairs={{0,1},{1,0},{2,3},{3,2},{4,5},{5,4},{6,7},{7,6},{8,9},{9,8},{10,11... | collective-permute-start | bytes 8650760 | tf_op jit(solution)/shard_map/ppermute | solution.py:97
  34.3 170.5 %collective-permute-start.2 = (bf16[1408,1024]{1,0:T(8,128)(2,1)}, bf16[1408,1024]{1,0:T(8,128)(2,1)}, u32[]{:S(2)}, u32[]{:S(2)}) collective-permute-start(bf16[1408,1024]{1,0:T(8,128)(2,1)} %bitcast.81), channel_id=1, source_target_pairs={{0,1},{1,0},{2,3},{3,2},{4,5},{5,4},{6,7},{7,6},{8,9},{9,8},{10,11... | collective-permute-start | bytes 8650760 | tf_op jit(solution)/shard_map/ppermute | solution.py:97
  37.1 167.7 %all-to-all-start = ((f32[16,1,128]{2,1,0:T(1,128)}), f32[16,1,128]{2,1,0:T(1,128)S(1)}, u32[]{:S(2)}, u32[]{:S(2)}) async-start(f32[16,1,128]{2,1,0:T(1,128)} %bitcast.9), calls=%async_computation | async-start | bytes 16384 | tf_op jit(solution)/shard_map/all_to_all | solution.py:131
  42.7 384.6 %reduce-scatter.4.cloned.1.call-start = ((), (), s32[]{:S(2)}) async-start(), calls=%async_computation.5 | async-start | bytes 8912896 | tf_op jit(solution)/shard_map/reduce_scatter | solution.py:170
  61.9 102.6 %copy-start.4 = (bf16[1,2048,704]{1,2,0:T(8,128)(2,1)S(1)}, bf16[1,2048,704]{1,2,0:T(8,128)(2,1)}, u32[]{:S(2)}) copy-start(bf16[1,2048,704]{1,2,0:T(8,128)(2,1)} %param.12) | copy-start | bytes 8650756
  64.7 170.4 %collective-permute-start.3 = (bf16[256,2048]{0,1:T(8,128)(2,1)}, bf16[256,2048]{0,1:T(8,128)(2,1)}, u32[]{:S(2)}, u32[]{:S(2)}) collective-permute-start(bf16[256,2048]{0,1:T(8,128)(2,1)} %broadcast_select_fusion), channel_id=1, source_target_pairs={{0,1},{1,0},{2,3},{3,2},{4,5},{5,4},{6,7},{7,6},{8,9},{9,8},{10,11... | collective-permute-start | bytes 3145736 | tf_op jit(solution)/shard_map/ppermute | solution.py:97
  164.5 11.5 %copy-start.3 = (bf16[2048,2048]{1,0:T(8,128)(2,1)S(1)}, bf16[2048,2048]{1,0:T(8,128)(2,1)}, u32[]{:S(2)}) copy-start(bf16[2048,2048]{1,0:T(8,128)(2,1)} %all-gather.4.cloned.1.call-done) | copy-start | bytes 25165828
  164.5 11.5 %copy-start.5 = (bf16[1,2048,704]{1,2,0:T(8,128)(2,1)S(1)}, bf16[1,2048,704]{1,2,0:T(8,128)(2,1)}, u32[]{:S(2)}) copy-start(bf16[1,2048,704]{1,2,0:T(8,128)(2,1)} %param.13) | copy-start | bytes 8650756
  194.8 10.0 %copy-start.6 = (bf16[1,1408,1024]{2,1,0:T(8,128)(2,1)S(1)}, bf16[1,1408,1024]{2,1,0:T(8,128)(2,1)}, u32[]{:S(2)}) copy-start(bf16[1,1408,1024]{2,1,0:T(8,128)(2,1)} %param.14) | copy-start | bytes 8650756
  204.8 11.5 %copy-start.7 = (bf16[2048,704]{0,1:T(8,128)(2,1)S(1)}, bf16[2048,704]{0,1:T(8,128)(2,1)}, u32[]{:S(2)}) copy-start(bf16[2048,704]{0,1:T(8,128)(2,1)} %fusion) | copy-start | bytes 8650756
  204.8 11.5 %copy-start.8 = (bf16[2048,704]{0,1:T(8,128)(2,1)S(1)}, bf16[2048,704]{0,1:T(8,128)(2,1)}, u32[]{:S(2)}) copy-start(bf16[2048,704]{0,1:T(8,128)(2,1)} %fusion.4) | copy-start | bytes 8650756
  226.5 8.6 %copy-start.2 = (bf16[512,2048]{0,1:T(8,128)(2,1)S(1)}, bf16[512,2048]{0,1:T(8,128)(2,1)}, u32[]{:S(2)}) copy-start(bf16[512,2048]{0,1:T(8,128)(2,1)} %convolution_convert_fusion) | copy-start | bytes 6291460
  250.4 176.9 %copy-start.1 = (bf16[704,2048]{1,0:T(8,128)(2,1)S(1)}, bf16[704,2048]{1,0:T(8,128)(2,1)}, u32[]{:S(2)}) copy-start(bf16[704,2048]{1,0:T(8,128)(2,1)} %param.17) | copy-start | bytes 8650756
Sparse Core Ops, SparseCore 0:
  8.9 23.9 all-gather.5
  34.5 14.4 all-gather.7
  51.7 112.8 all-gather.3
  250.6 176.6 reduce-scatter.3

commit v2 on v1

--- a/solution.py
+++ b/solution.py
@@ -1,7 +1,13 @@
+import functools
+
 import jax
 import jax.numpy as jnp
 from jax import lax
+from jax.experimental import pallas as pl
+from jax.experimental.pallas import tpu as pltpu
 from jax.sharding import PartitionSpec as P
+
+MESH = pl.DeviceIdType.MESH
 
 
 def from_partner(block, axis, distance):
@@ -93,13 +99,223 @@
     ).astype(jnp.float32)
     return (routed + shared_out).astype(tokens.dtype)
 
-def swap_cores(block):
-    return lax.ppermute(block, "core", [(0, 1), (1, 0)])
-
-
-def both_halves(block, core):
-    other = swap_cores(block)
-    return jnp.where(core == 0, block, other), jnp.where(core == 0, other, block)
+
+def place():
+    node, chip, core = lax.axis_index("node"), lax.axis_index("chip"), lax.axis_index("core")
+    return node // 2, node % 2, chip, core
+
+
+def near(z, x, y, core, first):
+    along_x = 1 - core if first else core
+    return (z * 2 + x + along_x * (1 - 2 * x), y + (1 - along_x) * (1 - 2 * y), core)
+
+
+def slot_of(z, x, y, core, p_other, q_other):
+    x_other = p_other * (1 - core) + q_other * core
+    y_other = p_other * core + q_other * (1 - core)
+    return z * 4 + (x + x_other * (1 - 2 * x)) * 2 + y + y_other * (1 - 2 * y)
+
+
+def greet(devices):
+    barrier = pltpu.get_barrier_semaphore()
+    for device in devices:
+        pl.semaphore_signal(barrier, inc=1, device_id=device, device_id_type=MESH)
+    pl.semaphore_wait(barrier, len(devices))
+
+
+def gather_kernel(line, parts, *refs):
+    tokens = refs[0]
+    weights = refs[1 : 1 + parts]
+    gathered = refs[1 + parts]
+    both = refs[2 + parts : 2 + 2 * parts]
+    own_sem, send_sem, recv_sem, keep_sem, weight_send, weight_recv = refs[2 + 2 * parts :]
+    z, x, y, core = place()
+    p_device, q_device = near(z, x, y, core, True), near(z, x, y, core, False)
+    partner = (z * 2 + x, y, 1 - core)
+    lines = [(lax.rem(z + d, line) * 2 + x, y, core) for d in range(1, line)]
+    greet(lines + [p_device, q_device, partner])
+    me = slot_of(z, x, y, core, 0, 0)
+
+    def push(source, slot, count, device):
+        copy = pltpu.make_async_remote_copy(
+            src_ref=source,
+            dst_ref=gathered.at[slot],
+            send_sem=send_sem.at[count],
+            recv_sem=recv_sem.at[slot],
+            device_id=device,
+            device_id_type=MESH,
+        )
+        copy.start()
+        return copy
+
+    def arrived(slot):
+        pltpu.make_async_remote_copy(
+            src_ref=gathered.at[slot],
+            dst_ref=gathered.at[slot],
+            send_sem=send_sem.at[0],
+            recv_sem=recv_sem.at[slot],
+            device_id=q_device,
+            device_id_type=MESH,
+        ).wait_recv()
+
+    sent = []
+    sent.append(push(tokens, me, len(sent), q_device))
+    for device in lines:
+        sent.append(push(tokens, me, len(sent), device))
+    sent.append(push(tokens, me, len(sent), p_device))
+    own = pltpu.make_async_copy(tokens, gathered.at[me], own_sem)
+    own.start()
+    moved, kept = [], []
+    for at in range(parts):
+        copy = pltpu.make_async_remote_copy(
+            src_ref=weights[at],
+            dst_ref=both[at].at[core],
+            send_sem=weight_send.at[at],
+            recv_sem=weight_recv.at[at],
+            device_id=partner,
+            device_id_type=MESH,
+        )
+        copy.start()
+        moved.append(copy)
+        keep = pltpu.make_async_copy(weights[at], both[at].at[core], keep_sem.at[at])
+        keep.start()
+        kept.append(keep)
+    for d in [*range(1, line, 2), *range(2, line, 2)]:
+        slot = slot_of(lax.rem(z + d, line), x, y, core, 0, 0)
+        arrived(slot)
+        sent.append(push(gathered.at[slot], slot, len(sent), q_device))
+        sent.append(push(gathered.at[slot], slot, len(sent), p_device))
+    for d in [0, *range(1, line, 2), *range(2, line, 2)]:
+        slot = slot_of(lax.rem(z + d, line), x, y, core, 1, 0)
+        arrived(slot)
+        sent.append(push(gathered.at[slot], slot, len(sent), q_device))
+    for p_other in (0, 1):
+        for d in range(line):
+            arrived(slot_of(lax.rem(z + d, line), x, y, core, p_other, 1))
+    for copy in sent:
+        copy.wait_send()
+    own.wait()
+    for at in range(parts):
+        moved[at].wait()
+        kept[at].wait()
+
+
+def gather_plane(tokens, weights):
+    chips = lax.axis_size("node") * lax.axis_size("chip")
+    parts = len(weights)
+    anywhere = pl.BlockSpec(memory_space=pl.ANY)
+    shapes = [jax.ShapeDtypeStruct((chips, *tokens.shape), tokens.dtype)]
+    shapes += [jax.ShapeDtypeStruct((2, *w.shape), w.dtype) for w in weights]
+    return pl.pallas_call(
+        functools.partial(gather_kernel, chips // 4, parts),
+        out_shape=shapes,
+        in_specs=[anywhere] * (1 + parts),
+        out_specs=[anywhere] * (1 + parts),
+        scratch_shapes=[
+            pltpu.SemaphoreType.DMA,
+            pltpu.SemaphoreType.DMA((chips - 1,)),
+            pltpu.SemaphoreType.DMA((chips,)),
+            pltpu.SemaphoreType.DMA((parts,)),
+            pltpu.SemaphoreType.DMA((parts,)),
+            pltpu.SemaphoreType.DMA((parts,)),
+        ],
+        compiler_params=pltpu.CompilerParams(collective_id=0, has_side_effects=True),
+    )(tokens, *weights)
+
+
+def reduce_kernel(line, terms, out, held, from_q, from_p, from_z, send_sem, q_sem, p_sem, z_sem):
+    z, x, y, core = place()
+    p_device, q_device = near(z, x, y, core, True), near(z, x, y, core, False)
+    lines = [(lax.rem(z + d, line) * 2 + x, y, core) for d in range(1, line)]
+    greet(lines + [p_device, q_device])
+    turn = [*range(1, line), 0]
+
+    def push(source, target, sem, count, device):
+        copy = pltpu.make_async_remote_copy(
+            src_ref=source,
+            dst_ref=target,
+            send_sem=send_sem.at[count],
+            recv_sem=sem,
+            device_id=device,
+            device_id_type=MESH,
+        )
+        copy.start()
+        return copy
+
+    def add_up(target, sources):
+        def step(i, carry):
+            rows = pl.ds(pl.multiple_of(i * 16, 16), 16)
+            total = sources[0][rows, :].astype(jnp.float32)
+            for source in sources[1:]:
+                total = total + source[rows, :].astype(jnp.float32)
+            target[rows, :] = total.astype(target.dtype)
+            return carry
+
+        lax.fori_loop(0, out.shape[0] // 16, step, 0)
+
+    sent, q_copies, p_copies, z_copies = [], {}, {}, {}
+    for p_other in (1, 0):
+        for d in turn:
+            slot = slot_of(lax.rem(z + d, line), x, y, core, p_other, 1)
+            at = p_other * line + d
+            copy = push(terms.at[slot], from_q.at[at], q_sem.at[at], len(sent), q_device)
+            sent.append(copy)
+            q_copies[p_other, d] = copy
+    for d in turn:
+        at = line + d
+        slot = slot_of(lax.rem(z + d, line), x, y, core, 1, 0)
+        q_copies[1, d].wait_recv()
+        add_up(held.at[at], [terms.at[slot], from_q.at[at]])
+        p_copies[d] = push(held.at[at], from_p.at[d], p_sem.at[d], len(sent), p_device)
+        sent.append(p_copies[d])
+    for d in turn:
+        slot = slot_of(lax.rem(z + d, line), x, y, core, 0, 0)
+        q_copies[0, d].wait_recv()
+        p_copies[d].wait_recv()
+        sources = [terms.at[slot], from_q.at[d], from_p.at[d]]
+        if d:
+            add_up(held.at[d], sources)
+            z_copies[d] = push(
+                held.at[d], from_z.at[d - 1], z_sem.at[d - 1], len(sent), lines[d - 1]
+            )
+            sent.append(z_copies[d])
+        else:
+            for other in range(1, line):
+                z_copies[other].wait_recv()
+            add_up(out, sources + [from_z.at[other - 1] for other in range(1, line)])
+    for copy in sent:
+        copy.wait_send()
+
+
+def reduce_plane(terms):
+    chips, rows, features = terms.shape
+    line = chips // 4
+    inside = pl.BlockSpec(memory_space=pltpu.VMEM)
+    return pl.pallas_call(
+        functools.partial(reduce_kernel, line),
+        out_shape=jax.ShapeDtypeStruct((rows, features), terms.dtype),
+        in_specs=[inside],
+        out_specs=inside,
+        scratch_shapes=[
+            pltpu.VMEM((2 * line, rows, features), terms.dtype),
+            pltpu.VMEM((2 * line, rows, features), terms.dtype),
+            pltpu.VMEM((line, rows, features), terms.dtype),
+            pltpu.VMEM((line - 1, rows, features), terms.dtype),
+            pltpu.SemaphoreType.DMA((chips - 1,)),
+            pltpu.SemaphoreType.DMA((2 * line,)),
+            pltpu.SemaphoreType.DMA((line,)),
+            pltpu.SemaphoreType.DMA((line - 1,)),
+        ],
+        compiler_params=pltpu.CompilerParams(
+            collective_id=1, has_side_effects=True, vmem_limit_bytes=40 << 20
+        ),
+    )(terms)
+
+
+def gated(rows, gate, up):
+    gate_out = jnp.dot(rows, gate, preferred_element_type=jnp.float32)
+    up_out = jnp.dot(rows, up, preferred_element_type=jnp.float32)
+    return (jax.nn.silu(gate_out) * up_out).astype(rows.dtype)
 
 
 def dense(
@@ -116,46 +332,32 @@
     rows, features = tokens.shape
     planes = ("node", "chip")
     chips = lax.axis_size("node") * lax.axis_size("chip")
-    group_chips = lax.axis_size("chip")
-    core = lax.axis_index("core")
-    chip = lax.axis_index("chip")
-    node = lax.axis_index("node")
-    expert = node * group_chips + chip
+    group_rows = lax.axis_size("chip") * rows
+    first = lax.axis_index("node") * group_rows
 
     codes = gate_codes.astype(jnp.float32)
     weights = codes / jnp.sum(codes, axis=1, keepdims=True)
     onehot = expert_ids[:, :, None] == jnp.arange(chips, dtype=jnp.int32)[None, None, :]
     table = jnp.sum(jnp.where(onehot, weights[:, :, None], 0.0), axis=1)
-
-    plane_rows = lax.all_gather(tokens, planes, axis=0, tiled=True)
-    share = lax.all_to_all(table.T.reshape(chips, 1, rows), planes, split_axis=0, concat_axis=0, tiled=True)
+    share = lax.all_to_all(
+        table.T.reshape(chips, 1, rows), planes, split_axis=0, concat_axis=0, tiled=True
+    )
     scale = share.reshape(-1, 1)
 
-    gate = both_halves(gate_halves[0], core)
-    up = both_halves(up_halves[0], core)
-    down = both_halves(down_halves[0], core)
-
-    group = lax.all_gather(lax.all_gather(tokens, "chip", axis=0, tiled=True), "core", axis=0, tiled=True)
-    shared_hidden = (
-        jax.nn.silu(jnp.dot(group, shared_gate, preferred_element_type=jnp.float32))
-        * jnp.dot(group, shared_up, preferred_element_type=jnp.float32)
-    ).astype(tokens.dtype)
-    shared_rows = jnp.dot(shared_hidden, shared_down, preferred_element_type=jnp.float32)
-    shared_rows = shared_rows.astype(tokens.dtype).reshape(2, group_chips * rows, features)
-    mine = jnp.where(core == 0, shared_rows[0], shared_rows[1])
-    theirs = jnp.where(core == 0, shared_rows[1], shared_rows[0])
-    shared_part = mine.astype(jnp.float32) + swap_cores(theirs).astype(jnp.float32)
-
-    hidden = jnp.concatenate(
-        [
-            (
-                jax.nn.silu(jnp.dot(plane_rows, gate[h], preferred_element_type=jnp.float32))
-                * jnp.dot(plane_rows, up[h], preferred_element_type=jnp.float32)
-            ).astype(tokens.dtype)
-            for h in (0, 1)
-        ],
-        axis=1,
-    )
+    plane_rows, gate, up, down, s_gate, s_up, s_down = gather_plane(
+        tokens,
+        (gate_halves[0], up_halves[0], down_halves[0], shared_gate, shared_up, shared_down),
+    )
+    plane_rows = plane_rows.reshape(chips * rows, features)
+
+    group = lax.dynamic_slice(plane_rows, (first, 0), (group_rows, features))
+    shared_part = sum(
+        jnp.dot(gated(group, s_gate[h], s_up[h]), s_down[h], preferred_element_type=jnp.float32)
+        .astype(tokens.dtype)
+        .astype(jnp.float32)
+        for h in (0, 1)
+    )
+    hidden = jnp.concatenate([gated(plane_rows, gate[h], up[h]) for h in (0, 1)], axis=1)
     out = jnp.concatenate(
         [
             (jnp.dot(hidden, down[h], preferred_element_type=jnp.float32) * scale).astype(tokens.dtype)
@@ -163,11 +365,10 @@
         ],
         axis=1,
     )
-    first = node * group_chips * rows
-    block = lax.dynamic_slice(out, (first, 0), (group_chips * rows, features))
+    block = lax.dynamic_slice(out, (first, 0), (group_rows, features))
     block = (block.astype(jnp.float32) + shared_part).astype(tokens.dtype)
     out = lax.dynamic_update_slice(out, block, (first, 0))
-    return lax.psum_scatter(out, planes, scatter_dimension=0, tiled=True)
+    return reduce_plane(out.reshape(chips, rows, features))
 
 
 def program(mesh, row, pieces, body):
@@ -194,7 +395,7 @@
     )
 
     def run(tokens, expert_ids, *others):
-        if experts <= 4 * expert_ids.shape[1]:
+        if mesh.shape["local"] == 4 and experts <= 4 * expert_ids.shape[1]:
             whole = program(fine, ("node", "chip", "core"), ("chip", "core"), dense)
         else:
             whole = program(mesh, ("node", "local"), "local", local)

time: 434 us -> 812 us (1.87); the launches traced: 434 us -> 803 us
  Pallas kernels: 0 us -> 666 us
  waiting for transfers between devices: 310 us -> 0.01 us
  local copies, waits for them, and re-layouts: 12.3 us -> 31.5 us
  between operations: 13.2 us -> 0.13 us
  matrix products: 74.9 us -> 85.7 us
    pallas_call x0 -> x2, Pallas kernels: none -> 666 us  [the longest x1 577 us: gather_plane(): pl.pallas_call(functools.partial(gather_kernel, chips // 4, parts), out_s...]
    reduce_scatter x1 -> x0, waiting for transfers between devices: 177 us -> none  [dense(): return lax.psum_scatter(out, planes, scatter_dimension=0, tiled=True)]
    all_gather x3 -> x0, waiting for transfers between devices: 131 us -> none  [the longest x1 99.6 us: dense(): plane_rows = lax.all_gather(tokens, planes, axis=0, tiled=True)]
    dynamic_update_slice x0 -> x1, local copies, waits for them, and re-layouts: none -> 12.3 us  [dense(): out = lax.dynamic_update_slice(out, block, (first, 0))]
    dot_general x6 -> x8, matrix products: 53.2 us -> 64.1 us  [the longest x4 26.5 us: gated(): gate_out = jnp.dot(rows, gate, preferred_element_type=jnp.float32)]
    unnamed x19 -> x25, local copies, waits for them, and re-layouts: 12.3 us -> 19.2 us
  transfers between devices with their start and end apart: 9 -> 1, of which waited for: 4 -> 0; matrix products, arithmetic and copies ran while one was open for 20% -> 9% of each run, Pallas kernels for 0% -> 72%
where the time goes in v2:
time: 812 us; the launch traced here: 803 us
  Pallas kernels  666 us (82%)
  matrix products  85.7 us (11%)
  local copies, waits for them, and re-layouts  31.5 us (4%)
  other arithmetic  11.3 us (1%)
  starting transfers between devices  8.31 us (1%)
    pallas_call x1, Pallas kernels, gather_plane(): pl.pallas_call(functools.partial(gather_kernel, chips // 4, parts), out_s...  577 us
    pallas_call x1, Pallas kernels, reduce_plane(): pl.pallas_call(functools.partial(reduce_kernel, line), out_shape=jax.Shap...  89.2 us
    dot_general x4, matrix products, gated(): gate_out = jnp.dot(rows, gate, preferred_element_type=jnp.float32)  26.5 us
    dot_general x2, matrix products, gated(): up_out = jnp.dot(rows, up, preferred_element_type=jnp.float32)  23.6 us
    dot_general x2, matrix products, dense(): jnp.dot(hidden, down[h], preferred_element_type=jnp.float32) * scale  21.6 us
    unnamed x25, local copies, waits for them, and re-layouts  19.2 us
  transfers between devices with their start and end apart: 1, of which 0 were waited for; matrix products, arithmetic and copies ran while one was open for 9% of the time, Pallas kernels for 72%

profile of v2, /device:TPU:0, one launch (start us, length us, event | category | flops | bytes accessed | tf_op | source)
XLA Modules:
  0.0 803.2 jit_solution(10391246878940837849)
XLA Ops:
  0.0 0.9 convert_reduce_fusion
  0.9 0.7 convert_divide_fusion
  1.6 1.3 select_reduce_fusion
  2.9 8.3 %all-to-all-start = ((f32[16,1,128]{2,1,0:T(1,128)}), f32[16,1,128]{2,1,0:T(1,128)S(1)}, u32[]{:S(2)}, u32[]{:S(2)}) async-start(f32[16,1,128]{2,1,0:T(1,128)} %bitcast.11), calls=%async_computation | async-start | bytes 16384 | tf_op jit(solution)/shard_map/all_to_all | solution.py:342
  11.2 4.6 copy.37
  15.8 0.0 copy-done.1
  15.8 2.8 copy.38
  18.6 4.8 copy.39.refs_4_
  23.4 0.0 copy-done.2
  23.4 2.8 copy.40.refs_5_
  26.2 577.0 %shard_map.91 = (bf16[16,128,2048]{2,1,0:T(8,128)(2,1)}, bf16[2,2048,704]{2,1,0:T(8,128)(2,1)}, bf16[2,2048,704]{2,1,0:T(8,128)(2,1)}, bf16[2,1408,1024]{2,1,0:T...) custom-call(bf16[128,2048]{1,0:T(8,128)(2,1)} %refs_0_.1, ...), custom_call_target="tpu_custom_call" | custom-call | tf_op jit(solution)/shard_map/pallas_call | solution.py:209
  603.2 0.0 copy-start.3
  603.2 0.0 copy-start.4
  603.2 11.3 %fusion.12 = f32[2048,704]{0,1:T(8,128)} fusion(bf16[2048,2048]{1,0:T(8,128)(2,1)} %bitcast.83, bf16[2,2048,704]{2,1,0:T(8,128)(2,1)} %get-tuple-element.13), kind=kOutput, calls=%fused_computation.20 | convolution fusion | flops 5905580032 | bytes 17301504 | tf_op jit(solution)/shard_map/dot_general | solution.py:316
  614.5 0.0 copy-done.3
  614.5 0.0 copy-done.4
  614.5 8.2 %fusion.9 = f32[2048,704]{0,1:T(8,128)} fusion(bf16[2048,2048]{1,0:T(8,128)(2,1)S(1)} %bitcast.90, bf16[2,2048,704]{2,1,0:T(8,128)(2,1)S(1)} %copy-done.4), kind=kOutput, calls=%fused_computation.17 | convolution fusion | flops 5905580032 | bytes 17301504 | tf_op jit(solution)/shard_map/dot_general | solution.py:316
  622.8 12.6 %multiply_convert_fusion.3 = bf16[2048,704]{0,1:T(8,128)(2,1)} fusion(f32[2048,704]{0,1:T(8,128)} %fusion.12, bf16[2048,2048]{1,0:T(8,128)(2,1)} %bitcast.84, bf16[2,2048,704]{2,1,0:T(8,128)(2,1)} %get-tuple-element.14), kind=kOutput, calls=%fused_computation.7 | convolution fusion | flops 5914230784 | bytes 20185088 | tf_op jit(solution)/shard_map/dot_general | solution.py:317
  635.4 0.0 copy-done.5
  635.4 11.0 %multiply_convert_fusion.2 = bf16[2048,704]{0,1:T(8,128)(2,1)} fusion(f32[2048,704]{0,1:T(8,128)S(1)} %copy-done.5, bf16[2048,2048]{1,0:T(8,128)(2,1)} %bitcast.85, bf16[2,2048,704]{2,1,0:T(8,128)(2,1)S(1)} %bitcast.94), kind=kOutput, calls=%fused_computation.6 | convolution fusion | flops 5914230784 | bytes 20185088 | tf_op jit(solution)/shard_map/dot_general | solution.py:317
  646.4 3.5 fusion.2
  649.9 6.4 fusion.50
  656.3 3.5 fusion.6
  659.8 0.0 all-to-all-done
  659.9 11.4 %multiply_convert_fusion.1 = bf16[2048,1024]{0,1:T(8,128)(2,1)} fusion(f32[2048]{0:T(1024)S(1)} %bitcast.91, bf16[2048,704]{0,1:T(8,128)(2,1)} %multiply_convert_fusion.2, bf16[2048,704]{0,1:T(8,128)(2,1)} %multiply_convert_fusion.3, bf16[2,1408,1024]{2,1,0:T(8,128)(2,1)} %get-tuple-element.15), kind=kOutput, calls=%fused_computation.4 | convolution fusion | flops 5921308672 | bytes 12853248 | tf_op jit(solution)/shard_map/dot_general | solution.py:363
  671.3 10.2 %multiply_convert_fusion = bf16[2048,1024]{0,1:T(8,128)(2,1)} fusion(f32[2048]{0:T(1024)S(1)} %bitcast.92, bf16[2048,704]{0,1:T(8,128)(2,1)S(1)} %copy-done.7, bf16[2048,704]{0,1:T(8,128)(2,1)S(1)} %copy-done.6, bf16[2,1408,1024]{2,1,0:T(8,128)(2,1)} %get-tuple-element.15), kind=kOutput, calls=%fused_computation.3 | convolution fusion | flops 5921308672 | bytes 12853248 | tf_op jit(solution)/shard_map/dot_general | solution.py:363
  681.5 8.5 %pad_maximum_fusion = bf16[2048,2048]{0,1:T(8,128)(2,1)} fusion(bf16[2048,1024]{0,1:T(8,128)(2,1)} %multiply_convert_fusion, bf16[2048,1024]{0,1:T(8,128)(2,1)} %multiply_convert_fusion.1), kind=kLoop, calls=%fused_computation.1 | loop fusion | flops 16777216 | bytes 16777216 | tf_op jit(solution)/shard_map/concatenate | solution.py:361
  690.0 7.6 fusion.53
  697.5 12.3 %copy.44 = bf16[2048,2048]{1,0:T(8,128)(2,1)} copy(bf16[2048,2048]{0,1:T(8,128)(2,1)} %fusion.53) | data formatting | bytes 16777216 | tf_op jit(solution)/shard_map/dynamic_update_slice | solution.py:370
  709.8 3.4 copy-done
  713.2 89.2 %shard_map.92 = bf16[128,2048]{1,0:T(8,128)(2,1)S(1)} custom-call(bf16[16,128,2048]{2,1,0:T(8,128)(2,1)S(1)} %bitcast.79), custom_call_target="tpu_custom_call" | custom-call | tf_op jit(solution)/shard_map/pallas_call | solution.py:294
  802.4 0.8 copy.49
  (13 shorter events, 0.0 us)
Async XLA Ops:
  0.0 15.8 %copy-start.1 = (bf16[1,2048,704]{1,2,0:T(8,128)(2,1)S(1)}, bf16[1,2048,704]{1,2,0:T(8,128)(2,1)}, u32[]{:S(2)}) copy-start(bf16[1,2048,704]{1,2,0:T(8,128)(2,1)} %param.13) | copy-start | bytes 8650756
  2.9 657.0 %all-to-all-start = ((f32[16,1,128]{2,1,0:T(1,128)}), f32[16,1,128]{2,1,0:T(1,128)S(1)}, u32[]{:S(2)}, u32[]{:S(2)}) async-start(f32[16,1,128]{2,1,0:T(1,128)} %bitcast.11), calls=%async_computation | async-start | bytes 16384 | tf_op jit(solution)/shard_map/all_to_all | solution.py:342
  18.6 4.8 copy-start.2
  603.2 11.3 %copy-start.3 = (bf16[16,128,2048]{2,1,0:T(8,128)(2,1)S(1)}, bf16[16,128,2048]{2,1,0:T(8,128)(2,1)}, u32[]{:S(2)}) copy-start(bf16[16,128,2048]{2,1,0:T(8,128)(2,1)} %get-tuple-element.12) | copy-start | bytes 25165828
  603.2 11.3 %copy-start.4 = (bf16[2,2048,704]{2,1,0:T(8,128)(2,1)S(1)}, bf16[2,2048,704]{2,1,0:T(8,128)(2,1)}, u32[]{:S(2)}) copy-start(bf16[2,2048,704]{2,1,0:T(8,128)(2,1)} %get-tuple-element.13) | copy-start | bytes 17301508
  614.5 20.8 %slice-start = ((s8[6291456]{0:T(1024)(128)(4,1)}), s8[2097152]{0:T(1024)(128)(4,1)S(1)}, s32[]{:S(2)}) async-start(s8[6291456]{0:T(1024)(128)(4,1)} %bitcast.93), calls=%async_computation.1 | async-start | bytes 4194304
  622.8 12.6 %slice-start.1 = ((s8[6291456]{0:T(1024)(128)(4,1)}), s8[4194304]{0:T(1024)(128)(4,1)S(1)}, s32[]{:S(2)}) async-start(s8[6291456]{0:T(1024)(128)(4,1)} %bitcast.93), calls=%async_computation.2 | async-start | bytes 8388608
  622.8 12.6 %copy-start.5 = (f32[2048,704]{0,1:T(8,128)S(1)}, f32[2048,704]{0,1:T(8,128)}, u32[]{:S(2)}) copy-start(f32[2048,704]{0,1:T(8,128)} %fusion.9) | copy-start | bytes 17301508
  659.8 11.5 %copy-start.6 = (bf16[2048,704]{0,1:T(8,128)(2,1)S(1)}, bf16[2048,704]{0,1:T(8,128)(2,1)}, u32[]{:S(2)}) copy-start(bf16[2048,704]{0,1:T(8,128)(2,1)} %multiply_convert_fusion.3) | copy-start | bytes 8650756
  659.9 11.4 %copy-start.7 = (bf16[2048,704]{0,1:T(8,128)(2,1)S(1)}, bf16[2048,704]{0,1:T(8,128)(2,1)}, u32[]{:S(2)}) copy-start(bf16[2048,704]{0,1:T(8,128)(2,1)} %multiply_convert_fusion.2) | copy-start | bytes 8650756
  709.8 3.4 copy-start
